TPU v7x, 128 devices: a whole 4x4x4 slice. The times are simulated.
128 devices in a mesh: row: 8 (over x, core), col: 16 (over y, z).
Axes of the slice: x: 4, y: 4, z: 4, core: 2. Of those that a mesh axis runs over, the one named last changes fastest.
Arguments:
- factor: float32 [4, 8, 1024, 2048], P(None, 'row', None, 'col'), as said below
- cross_cov: float32 [4, 8, 1024, 1024], P(None, 'row', 'col'), may hold values from -6 to 6
Outputs:
- overwritten: float32 [4, 8, 1024, 1024], P(None, 'row', 'col')
Inputs may be any that keep to these rules, and one draw needn't show every extreme that they name: The diagonal entries of the factor lie between 1 and 3.
All inputs are finite; a program needn't handle non-finite values.
Results may differ from a plain program's by a relative error of at most 0.00014.
Values sent between devices are 32-bit elements; how exact they have to be, the bound alone decides.
No kernel may reach another device: no remote copies, remote signals or barrier semaphores. Data moves between devices by JAX's collectives and lax.ppermute only.
A program may use at most 128 MiB of HBM per device.

v0:
```python
import jax
import jax.numpy as jnp
from jax import lax
from jax.sharding import PartitionSpec as P


def broadcast(x, axis, root):
    mine = lax.axis_index(axis) == root
    return lax.psum(jnp.where(mine, x, jnp.zeros_like(x)), axis)


def spread(block, root):
    return broadcast(block, "row", root)


def reduce_turn(partial_value):
    return lax.psum_scatter(partial_value, "col", scatter_dimension=0, tiled=True)


def shards(factor, cross_cov):
    col_id = lax.axis_index("col")
    row_id = lax.axis_index("row")
    lead_rows = factor[0, 0]
    own_rhs = cross_cov[0, 0]
    block_row, block_rhs = (
        lax.all_gather(lead_rows, "col", axis=1, tiled=True),
        lax.all_gather(own_rhs, "col", axis=0, tiled=True),
    )
    block_size = block_row.shape[0]
    first_block = lax.linalg.triangular_solve(
        block_row[:, :block_size], block_rhs, left_side=True, lower=True
    )
    first_block = spread(first_block, 0)
    second_rhs = block_rhs - jnp.dot(
        block_row[:, :block_size], first_block, precision=lax.Precision.HIGHEST
    )
    second_block = lax.linalg.triangular_solve(
        block_row[:, block_size:], second_rhs, left_side=True, lower=True
    )
    second_block = spread(second_block, 1)
    solved = jnp.concatenate([first_block, second_block], 0)
    local_factor = factor[:, 0]
    col_width = local_factor.shape[2]
    my_rows = lax.dynamic_slice_in_dim(solved, col_id * col_width, col_width, 0)
    pieces = []
    for turn_id in range(local_factor.shape[0]):
        partial_value = jnp.dot(local_factor[turn_id], my_rows, precision=lax.Precision.HIGHEST)
        pieces.append(reduce_turn(partial_value))
    reduced = jnp.stack(pieces, 0)
    updated = cross_cov[:, 0] - reduced
    slice_rows = own_rhs.shape[0]
    first_piece = lax.dynamic_slice_in_dim(first_block, col_id * slice_rows, slice_rows, 0)
    second_piece = lax.dynamic_slice_in_dim(second_block, col_id * slice_rows, slice_rows, 0)
    head_rows = jnp.where(
        row_id == 0, first_piece, jnp.where(row_id == 1, second_piece, updated[0])
    )
    result = jnp.concatenate([head_rows[None], updated[1:]], 0)
    return result[:, None]


def solution(mesh):
    placed = (P(None, "row", None, "col"), P(None, "row", "col", None))
    return jax.shard_map(
        shards, mesh=mesh, in_specs=placed, out_specs=P(None, "row", "col", None), check_vma=False
    )
```

profile of v0, /device:TPU:0, one launch (start us, length us, event | category | flops | bytes accessed | tf_op | source)
XLA Modules:
  0.0 875.4 jit_solution(348379081481082438)
XLA Ops:
  10.5 53.1 %all-gather.7.cloned.1.call-done = f32[1,1,1024,1024]{3,1,0,2:T(1,128)} async-done(((f32[1,1,64,1024]{3,1,0,2:T(1,128)}), f32[1,1,1024,1024]{3,1,0,2:T(1,128)}) %all-gather.7.cloned.1.call-update) | async-done | bytes 4194320 | tf_op jit(solution)/shard_map/all_gather | solution.py:27
  63.7 11.0 %copy.10 = f32[1,1,1024,1024]{2,3,1,0:T(8,128)} copy(f32[1,1,1024,1024]{3,1,0,2:T(1,128)} %all-gather.7.cloned.1.call-done) | data formatting | bytes 8388608 | tf_op jit(solution)/shard_map/all_gather | solution.py:27
  74.7 69.2 %all-gather.5.cloned.1.call-done = f32[1,1,1024,2048]{3,2,1,0:T(8,128)} async-done(((f32[1,1,1024,128]{3,2,1,0:T(8,128)}), f32[1,1,1024,2048]{3,2,1,0:T(8,128)}) %all-gather.5.cloned.1.call-update) | async-done | bytes 8388624 | tf_op jit(solution)/shard_map/all_gather | solution.py:26
  143.9 8.0 slice_select_fusion
  151.9 22.5 %while.4 = (s32[]{:T(128)}, f32[1024,1024]{1,0:T(8,128)}, s32[8,2]{0,1:T(2,128)S(1)}, f32[8,128,128]{2,1,0:T(8,128)S(1)}, s32[]{:T(128)}) while((s32[]{:T(128)}, f32[1024,1024]{1,0:T(8,128)}, s32[8,2]{0,1:T(2,128)S(1)}, f32[8,128,128]{2,1,0:T(8,128)S(1)}, s32[]{:T(128)}) %tuple.80), condition=%wide.while_cond, body=%wide.while_body.sunk | while | flops 2 | bytes 131181 | solution.py:30
  174.4 78.8 %custom-call.4 = f32[8,128,128]{1,2,0:T(8,128)S(1)} custom-call(f32[8,128,128]{2,1,0:T(8,128)S(1)} %get-tuple-element.20), custom_call_target="InvertDiagBlocksLowerTriangular" | custom-call | tf_op jit(solution)/shard_map/triangular_solve/custom-call.1 | solution.py:30
  271.3 5.4 convolution_subtract_fusion.5
  277.4 6.0 convolution_subtract_fusion.3
  284.1 7.5 convolution_subtract_fusion.8
  294.8 22.5 %while.5 = (s32[]{:T(128)}, f32[1024,1024]{1,0:T(8,128)}, s32[8,2]{0,1:T(2,128)S(1)}, f32[8,128,128]{2,1,0:T(8,128)S(1)}, s32[]{:T(128)}) while((s32[]{:T(128)}, f32[1024,1024]{1,0:T(8,128)}, s32[8,2]{0,1:T(2,128)S(1)}, f32[8,128,128]{2,1,0:T(8,128)S(1)}, s32[]{:T(128)}) %tuple.102), condition=%wide.while_cond.clone, body=%wide.while_body.clone.sunk | while | flops 2 | bytes 131181 | solution.py:37
  317.3 78.6 %custom-call.5 = f32[8,128,128]{1,2,0:T(8,128)S(1)} custom-call(f32[8,128,128]{2,1,0:T(8,128)S(1)} %get-tuple-element.21), custom_call_target="InvertDiagBlocksLowerTriangular" | custom-call | tf_op jit(solution)/shard_map/triangular_solve/custom-call.1 | solution.py:37
  395.9 30.9 %bitcast_subtract_fusion = f32[1024,1024]{0,1:T(8,128)S(1)} fusion(f32[1024,1024]{1,0:T(8,128)} %all-reduce.3.cloned.1.call-done, f32[1024,2048]{1,0:T(8,128)} %bitcast.173, f32[1,1,1024,1024]{2,3,1,0:T(8,128)} %copy.10), kind=kOutput, calls=%fused_computation.7 | convolution fusion | flops 12885950464 | bytes 16777216 | tf_op jit(solution)/shard_map/dot_general | solution.py:34
  443.5 5.4 convolution_subtract_fusion.4
  449.5 6.2 convolution_subtract_fusion.2
  456.3 7.3 convolution_subtract_fusion.6
  466.9 71.9 %all-reduce.5.cloned.1.call-done = f32[1024,1024]{1,0:T(8,128)} async-done(((f32[1024,1024]{1,0:T(8,128)}), f32[1024,1024]{1,0:T(8,128)}) %all-reduce.5.cloned.1.call-update) | async-done | bytes 4194320 | tf_op jit(solution)/shard_map/psum | solution.py:9
  538.8 6.2 convolution_bitcast_fusion.3
  545.1 6.1 convolution_bitcast_fusion.2
  551.3 6.1 convolution_bitcast_fusion.1
  557.5 6.2 convolution_bitcast_fusion
  563.7 59.3 %reduce-scatter.5.cloned.1.call-done = f32[64,1024]{1,0:T(8,128)} async-done(((f32[1024,1024]{1,0:T(8,128)}), f32[64,1024]{1,0:T(8,128)}) %reduce-scatter.5.cloned.1.call-update) | async-done | bytes 262160 | tf_op jit(solution)/shard_map/reduce_scatter | solution.py:17
  623.1 80.6 %reduce-scatter.7.cloned.1.call-done = f32[64,1024]{1,0:T(8,128)} async-done(((f32[1024,1024]{1,0:T(8,128)}), f32[64,1024]{1,0:T(8,128)}) %reduce-scatter.7.cloned.1.call-update) | async-done | bytes 262160 | tf_op jit(solution)/shard_map/reduce_scatter | solution.py:17
  703.7 80.4 %reduce-scatter.9.cloned.1.call-done = f32[64,1024]{1,0:T(8,128)} async-done(((f32[1024,1024]{1,0:T(8,128)}), f32[64,1024]{1,0:T(8,128)}) %reduce-scatter.9.cloned.1.call-update) | async-done | bytes 262160 | tf_op jit(solution)/shard_map/reduce_scatter | solution.py:17
  784.0 80.7 %reduce-scatter.11.cloned.1.call-done = f32[64,1024]{1,0:T(8,128)} async-done(((f32[1024,1024]{1,0:T(8,128)}), f32[64,1024]{1,0:T(8,128)}) %reduce-scatter.11.cloned.1.call-update) | async-done | bytes 262160 | tf_op jit(solution)/shard_map/reduce_scatter | solution.py:17
  (108 shorter events, 96.1 us)
Async XLA Ops:
  6.5 57.1 %all-gather.7.cloned.1.call-start = ((), (), s32[]{:S(2)}) async-start(), calls=%async_computation.11 | async-start | bytes 4456448 | tf_op jit(solution)/shard_map/all_gather | solution.py:27
  8.5 135.4 %all-gather.5.cloned.1.call-start = ((), (), s32[]{:S(2)}) async-start(), calls=%async_computation.10 | async-start | bytes 8912896 | tf_op jit(solution)/shard_map/all_gather | solution.py:26
  10.5 385.5 %all-reduce.3.cloned.1.call-start = ((), (), s32[]{:S(2)}) async-start(), calls=%async_computation.4 | async-start | bytes 8388608 | tf_op jit(solution)/shard_map/psum | solution.py:9
  253.2 4.8 copy-start
  294.7 244.1 %all-reduce.5.cloned.1.call-start = ((), (), s32[]{:S(2)}) async-start(), calls=%async_computation.5 | async-start | bytes 8388608 | tf_op jit(solution)/shard_map/psum | solution.py:9
  466.8 72.0 %copy-start.1 = (f32[4,1,1024,128]{3,2,1,0:T(8,128)S(1)}, f32[4,1,1024,128]{3,2,1,0:T(8,128)}, u32[]{:S(2)}) copy-start(f32[4,1,1024,128]{3,2,1,0:T(8,128)} %param.4) | copy-start | bytes 6291460
  466.8 156.2 %reduce-scatter.5.cloned.1.call-start = ((), (), s32[]{:S(2)}) async-start(), calls=%async_computation.6 | async-start | bytes 4456448 | tf_op jit(solution)/shard_map/reduce_scatter | solution.py:17
  545.0 158.6 %reduce-scatter.7.cloned.1.call-start = ((), (), s32[]{:S(2)}) async-start(), calls=%async_computation.7 | async-start | bytes 4456448 | tf_op jit(solution)/shard_map/reduce_scatter | solution.py:17
  551.2 232.8 %reduce-scatter.9.cloned.1.call-start = ((), (), s32[]{:S(2)}) async-start(), calls=%async_computation.8 | async-start | bytes 4456448 | tf_op jit(solution)/shard_map/reduce_scatter | solution.py:17
  557.4 307.3 %reduce-scatter.11.cloned.1.call-start = ((), (), s32[]{:S(2)}) async-start(), calls=%async_computation.9 | async-start | bytes 4456448 | tf_op jit(solution)/shard_map/reduce_scatter | solution.py:17
  563.7 301.1 %copy-start.2 = (f32[4,1,64,1024]{3,2,1,0:T(8,128)S(1)}, f32[4,1,64,1024]{3,2,1,0:T(8,128)}, u32[]{:S(2)}) copy-start(f32[4,1,64,1024]{3,2,1,0:T(8,128)} %param.5) | copy-start | bytes 3145732
Sparse Core Ops, SparseCore 0:
  9.5 54.1 all-gather.6
  65.8 78.0 all-gather.4
  294.9 73.0 all-reduce.2
  467.0 71.7 all-reduce.4
  545.1 77.8 reduce-scatter.4
  626.6 77.0 reduce-scatter.6
  707.0 76.9 reduce-scatter.8
  787.7 77.0 reduce-scatter.10
where the time goes:
time: 880 us; the launch traced here: 875 us
  waiting for transfers between devices  495 us (56%)
  other arithmetic  174 us (20%)
  matrix products  132 us (15%)
  local copies, waits for them, and re-layouts  59.6 us (7%)
  between operations  14.1 us (2%)
    reduce_scatter x4, waiting for transfers between devices, reduce_turn(): lax.psum_scatter(partial_value, 'col', scatter_dimension=0, tiled=True)  301 us
    another operation x2, other arithmetic, shards(): lax.linalg.triangular_solve(block_row[:, block_size:], second_rhs, left_s...  86.6 us
    another operation x2, other arithmetic, shards(): lax.linalg.triangular_solve(block_row[:, :block_size], block_rhs, left_si...  78.8 us
    psum x2, waiting for transfers between devices, broadcast(): return lax.psum(jnp.where(mine, x, jnp.zeros_like(x)), axis)  71.9 us
    all_gather x1, waiting for transfers between devices, shards(): lax.all_gather(lead_rows, 'col', axis=1, tiled=True)  69.2 us
    all_gather x1, waiting for transfers between devices, shards(): lax.all_gather(own_rhs, 'col', axis=0, tiled=True)  53.1 us
    another operation x15, matrix products, shards(): lax.linalg.triangular_solve(block_row[:, :block_size], block_rhs, left_si...  38.9 us
    another operation x15, matrix products, shards(): lax.linalg.triangular_solve(block_row[:, block_size:], second_rhs, left_s...  37.4 us
  transfers between devices with their start and end apart: 8, of which 7 were waited for; matrix products, arithmetic and copies ran while one was open for 15% of the time, Pallas kernels for 0%

commit v1 on v0

--- a/solution.py
+++ b/solution.py
@@ -6,7 +6,7 @@
 
 def broadcast(x, axis, root):
     mine = lax.axis_index(axis) == root
-    return lax.psum(jnp.where(mine, x, jnp.zeros_like(x)), axis)
+    return jnp.sum(lax.all_gather(jnp.where(mine, x, jnp.zeros_like(x)), axis), axis=0)
 
 
 def spread(block, root):

time: 880 us -> 1060 us (1.20)
  waiting for transfers between devices: 495 us -> 618 us
  other arithmetic: 174 us -> 203 us
  local copies, waits for them, and re-layouts: 59.6 us -> 83.5 us
    all_gather x0 -> x2, waiting for transfers between devices: none -> 211 us  [broadcast(): lax.all_gather(jnp.where(mine, x, jnp.zeros_like(x)), axis)]
    psum x2 -> x0, waiting for transfers between devices: 71.9 us -> none  [broadcast(): return lax.psum(jnp.where(mine, x, jnp.zeros_like(x)), axis)]
    reduce_sum x0 -> x2, other arithmetic: none -> 29.4 us  [broadcast(): jnp.sum(lax.all_gather(jnp.where(mine, x, jnp.zeros_like(x)), axis), axis=0)]
    unnamed x7 -> x11, local copies, waits for them, and re-layouts: 0.99 us -> 22.6 us
    reduce_scatter x4, waiting for transfers between devices: 301 us -> 285 us  [reduce_turn(): lax.psum_scatter(partial_value, 'col', scatter_dimension=0, tiled=True)]
  transfers between devices with their start and end apart: 8 -> 8, of which waited for: 7 -> 8; matrix products, arithmetic and copies ran while one was open for 15% -> 14% of each run, Pallas kernels for 0% -> 0%
where the time goes in v1:
time: 1060 us; the launch traced here: 1050 us
  waiting for transfers between devices  618 us (58%)
  other arithmetic  203 us (19%)
  matrix products  132 us (12%)
  local copies, waits for them, and re-layouts  83.5 us (8%)
  between operations  14.1 us (1%)
    reduce_scatter x4, waiting for transfers between devices, reduce_turn(): lax.psum_scatter(partial_value, 'col', scatter_dimension=0, tiled=True)  285 us
    all_gather x2, waiting for transfers between devices, broadcast(): lax.all_gather(jnp.where(mine, x, jnp.zeros_like(x)), axis)  211 us
    another operation x2, other arithmetic, shards(): lax.linalg.triangular_solve(block_row[:, block_size:], second_rhs, left_s...  86.6 us
    another operation x2, other arithmetic, shards(): lax.linalg.triangular_solve(block_row[:, :block_size], block_rhs, left_si...  78.8 us
    all_gather x1, waiting for transfers between devices, shards(): lax.all_gather(lead_rows, 'col', axis=1, tiled=True)  69.3 us
    all_gather x1, waiting for transfers between devices, shards(): lax.all_gather(own_rhs, 'col', axis=0, tiled=True)  53.1 us
    another operation x15, matrix products, shards(): lax.linalg.triangular_solve(block_row[:, :block_size], block_rhs, left_si...  38.9 us
    another operation x15, matrix products, shards(): lax.linalg.triangular_solve(block_row[:, block_size:], second_rhs, left_s...  37.4 us
  transfers between devices with their start and end apart: 8, of which 8 were waited for; matrix products, arithmetic and copies ran while one was open for 14% of the time, Pallas kernels for 0%

profile of v1, /device:TPU:0, one launch (start us, length us, event | category | flops | bytes accessed | tf_op | source)
XLA Modules:
  0.0 1051.9 jit_solution(94198582108374440)
XLA Ops:
  10.5 53.1 %all-gather.11.cloned.1.call-done = f32[1,1,1024,1024]{3,1,0,2:T(1,128)} async-done(((f32[1,1,64,1024]{3,1,0,2:T(1,128)}), f32[1,1,1024,1024]{3,1,0,2:T(1,128)}) %all-gather.11.cloned.1.call-update) | async-done | bytes 4194320 | tf_op jit(solution)/shard_map/all_gather | solution.py:27
  63.7 11.0 %copy.7 = f32[1,1,1024,1024]{2,3,1,0:T(8,128)} copy(f32[1,1,1024,1024]{3,1,0,2:T(1,128)} %all-gather.11.cloned.1.call-done) | data formatting | bytes 8388608 | tf_op jit(solution)/shard_map/all_gather | solution.py:27
  74.6 69.3 %all-gather.9.cloned.1.call-done = f32[1,1,1024,2048]{3,2,1,0:T(8,128)} async-done(((f32[1,1,1024,128]{3,2,1,0:T(8,128)}), f32[1,1,1024,2048]{3,2,1,0:T(8,128)}) %all-gather.9.cloned.1.call-update) | async-done | bytes 8388624 | tf_op jit(solution)/shard_map/all_gather | solution.py:26
  143.9 8.0 slice_select_fusion
  151.9 24.1 %while.4 = (s32[]{:T(128)}, f32[1024,1024]{1,0:T(8,128)}, s32[8,2]{0,1:T(2,128)S(1)}, f32[8,128,128]{2,1,0:T(8,128)S(1)}, s32[]{:T(128)}) while((s32[]{:T(128)}, f32[1024,1024]{1,0:T(8,128)}, s32[8,2]{0,1:T(2,128)S(1)}, f32[8,128,128]{2,1,0:T(8,128)S(1)}, s32[]{:T(128)}) %tuple.80), condition=%wide.while_cond, body=%wide.while_body.sunk | while | flops 2 | bytes 131181 | solution.py:30
  176.1 78.8 %custom-call.4 = f32[8,128,128]{1,2,0:T(8,128)S(1)} custom-call(f32[8,128,128]{2,1,0:T(8,128)S(1)} %get-tuple-element.20), custom_call_target="InvertDiagBlocksLowerTriangular" | custom-call | tf_op jit(solution)/shard_map/triangular_solve/custom-call.1 | solution.py:30
  285.8 7.5 convolution_subtract_fusion.8
  296.4 23.1 %while.5 = (s32[]{:T(128)}, f32[1024,1024]{1,0:T(8,128)}, s32[8,2]{0,1:T(2,128)S(1)}, f32[8,128,128]{2,1,0:T(8,128)S(1)}, s32[]{:T(128)}) while((s32[]{:T(128)}, f32[1024,1024]{1,0:T(8,128)}, s32[8,2]{0,1:T(2,128)S(1)}, f32[8,128,128]{2,1,0:T(8,128)S(1)}, s32[]{:T(128)}) %tuple.102), condition=%wide.while_cond.clone, body=%wide.while_body.clone.sunk | while | flops 2 | bytes 131181 | solution.py:37
  319.5 78.6 %custom-call.5 = f32[8,128,128]{1,2,0:T(8,128)S(1)} custom-call(f32[8,128,128]{2,1,0:T(8,128)S(1)} %get-tuple-element.21), custom_call_target="InvertDiagBlocksLowerTriangular" | custom-call | tf_op jit(solution)/shard_map/triangular_solve/custom-call.1 | solution.py:37
  398.1 53.5 %all-gather.13.cloned.1.call-done = f32[8192,1024]{1,0:T(8,128)} async-done(((f32[1024,1024]{1,0:T(8,128)}), f32[8192,1024]{1,0:T(8,128)}) %all-gather.13.cloned.1.call-update) | async-done | bytes 33554448 | tf_op jit(solution)/shard_map/all_gather | solution.py:9
  451.6 14.6 %reduce_sum.18 = f32[1024,1024]{1,0:T(8,128)} reduce(f32[8,1024,1024]{2,1,0:T(8,128)} %bitcast.170, f32[]{:T(128)} %constant.22.clone.1), dimensions={0}, to_apply=%region_0.0 | reduce | flops 7340032 | bytes 37748740 | tf_op jit(solution)/shard_map/reduce_sum | solution.py:9
  466.2 30.8 %bitcast_subtract_fusion = f32[1024,1024]{0,1:T(8,128)S(1)} fusion(f32[1024,1024]{1,0:T(8,128)} %reduce_sum.18, f32[1024,2048]{1,0:T(8,128)} %bitcast.181, f32[1,1,1024,1024]{2,3,1,0:T(8,128)} %copy.7), kind=kOutput, calls=%fused_computation.7 | convolution fusion | flops 12885950464 | bytes 16777216 | tf_op jit(solution)/shard_map/dot_general | solution.py:34
  519.8 6.1 convolution_subtract_fusion.2
  526.6 7.3 convolution_subtract_fusion.6
  537.2 157.0 %all-gather.15.cloned.1.call-done = f32[8192,1024]{1,0:T(8,128)} async-done(((f32[1024,1024]{1,0:T(8,128)}), f32[8192,1024]{1,0:T(8,128)}) %all-gather.15.cloned.1.call-update) | async-done | bytes 33554448 | tf_op jit(solution)/shard_map/all_gather | solution.py:9
  694.2 14.8 %reduce_sum.19 = f32[1024,1024]{1,0:T(8,128)} reduce(f32[8,1024,1024]{2,1,0:T(8,128)} %bitcast.171, f32[]{:T(128)} %constant.22.clone.1), dimensions={0}, to_apply=%region_1.0 | reduce | flops 7340032 | bytes 37748740 | tf_op jit(solution)/shard_map/reduce_sum | solution.py:9
  709.0 6.1 convolution_bitcast_fusion.3
  720.6 6.2 convolution_bitcast_fusion.2
  732.2 6.4 convolution_bitcast_fusion.1
  744.2 6.2 convolution_bitcast_fusion
  755.9 43.7 %reduce-scatter.13.cloned.1.call-done = f32[64,1024]{1,0:T(8,128)} async-done(((f32[1024,1024]{1,0:T(8,128)}), f32[64,1024]{1,0:T(8,128)}) %reduce-scatter.13.cloned.1.call-update) | async-done | bytes 262160 | tf_op jit(solution)/shard_map/reduce_scatter | solution.py:17
  799.5 80.6 %reduce-scatter.15.cloned.1.call-done = f32[64,1024]{1,0:T(8,128)} async-done(((f32[1024,1024]{1,0:T(8,128)}), f32[64,1024]{1,0:T(8,128)}) %reduce-scatter.15.cloned.1.call-update) | async-done | bytes 262160 | tf_op jit(solution)/shard_map/reduce_scatter | solution.py:17
  880.1 80.4 %reduce-scatter.17.cloned.1.call-done = f32[64,1024]{1,0:T(8,128)} async-done(((f32[1024,1024]{1,0:T(8,128)}), f32[64,1024]{1,0:T(8,128)}) %reduce-scatter.17.cloned.1.call-update) | async-done | bytes 262160 | tf_op jit(solution)/shard_map/reduce_scatter | solution.py:17
  960.5 80.7 %reduce-scatter.19.cloned.1.call-done = f32[64,1024]{1,0:T(8,128)} async-done(((f32[1024,1024]{1,0:T(8,128)}), f32[64,1024]{1,0:T(8,128)}) %reduce-scatter.19.cloned.1.call-update) | async-done | bytes 262160 | tf_op jit(solution)/shard_map/reduce_scatter | solution.py:17
  (114 shorter events, 136.7 us)
Async XLA Ops:
  6.5 57.1 %all-gather.11.cloned.1.call-start = ((), (), s32[]{:S(2)}) async-start(), calls=%async_computation.5 | async-start | bytes 4456448 | tf_op jit(solution)/shard_map/all_gather | solution.py:27
  8.5 135.4 %all-gather.9.cloned.1.call-start = ((), (), s32[]{:S(2)}) async-start(), calls=%async_computation.4 | async-start | bytes 8912896 | tf_op jit(solution)/shard_map/all_gather | solution.py:26
  10.5 441.1 %all-gather.13.cloned.1.call-start = ((), (), s32[]{:S(2)}) async-start(), calls=%async_computation.6 | async-start | bytes 37748736 | tf_op jit(solution)/shard_map/all_gather | solution.py:9
  254.8 4.8 copy-start
  296.3 397.9 %all-gather.15.cloned.1.call-start = ((), (), s32[]{:S(2)}) async-start(), calls=%async_computation.7 | async-start | bytes 37748736 | tf_op jit(solution)/shard_map/all_gather | solution.py:9
  537.1 262.4 %reduce-scatter.13.cloned.1.call-start = ((), (), s32[]{:S(2)}) async-start(), calls=%async_computation.8 | async-start | bytes 4456448 | tf_op jit(solution)/shard_map/reduce_scatter | solution.py:17
  694.2 14.8 %copy-start.1 = (f32[4,1,1024,128]{3,2,1,0:T(8,128)S(1)}, f32[4,1,1024,128]{3,2,1,0:T(8,128)}, u32[]{:S(2)}) copy-start(f32[4,1,1024,128]{3,2,1,0:T(8,128)} %param.4) | copy-start | bytes 6291460
  720.6 159.6 %reduce-scatter.15.cloned.1.call-start = ((), (), s32[]{:S(2)}) async-start(), calls=%async_computation.9 | async-start | bytes 4456448 | tf_op jit(solution)/shard_map/reduce_scatter | solution.py:17
  732.2 228.3 %reduce-scatter.17.cloned.1.call-start = ((), (), s32[]{:S(2)}) async-start(), calls=%async_computation.10 | async-start | bytes 4456448 | tf_op jit(solution)/shard_map/reduce_scatter | solution.py:17
  744.1 297.1 %reduce-scatter.19.cloned.1.call-start = ((), (), s32[]{:S(2)}) async-start(), calls=%async_computation.11 | async-start | bytes 4456448 | tf_op jit(solution)/shard_map/reduce_scatter | solution.py:17
  755.8 285.4 %copy-start.2 = (f32[4,1,64,1024]{3,2,1,0:T(8,128)S(1)}, f32[4,1,64,1024]{3,2,1,0:T(8,128)}, u32[]{:S(2)}) copy-start(f32[4,1,64,1024]{3,2,1,0:T(8,128)} %param.5) | copy-start | bytes 3145732
Sparse Core Ops, SparseCore 0:
  9.5 54.1 all-gather.10
  65.8 78.0 all-gather.8
  296.4 155.1 all-gather.12
  537.2 156.8 all-gather.14
  720.7 78.7 reduce-scatter.12
  803.1 77.0 reduce-scatter.14
  883.5 76.9 reduce-scatter.16
  964.2 76.9 reduce-scatter.18
